TPU v7x, 32 devices: a whole 2x2x4 slice. The times are simulated.
32 devices in a mesh: grp: 2 (over x), seq: 16 (over z, y, core).
Axes of the slice: x: 2, y: 2, z: 4, core: 2. Of those that a mesh axis runs over, the one named last changes fastest.
Arguments:
- inputs: bfloat16 [4096, 4096], P(('grp', 'seq')), parts along dimension 0, may hold values from -6 to 6
- in_weight: bfloat16 [4096, 768], replicated, may hold values from -0.09375 to 0.09375
- filter_taps: float32 [2048, 256], P('seq'), may hold values from -6 to 6
- grad_out: bfloat16 [4096, 256], P(('grp', 'seq')), parts along dimension 0, may hold values from -6 to 6
Outputs:
- grad_inputs: bfloat16 [4096, 4096], P(('grp', 'seq')), parts along dimension 0
- grad_weight: float32 [8192, 768], P(('grp', 'seq')), parts along dimension 0
- grad_taps: float32 [4096, 256], P(('grp', 'seq')), parts along dimension 0
There are 2 independent parts, one for each index of `grp`. A program takes and returns all parts, laid end to end along the dimension named above; an argument that names none is the same for every part. Nothing has to cross between parts.
All inputs are finite; a program needn't handle non-finite values.
Results may differ from a plain program's by a relative error of at most 0.0064.
Values sent between devices are 32-bit elements; how exact they have to be, the bound alone decides.
A program may use at most 128 MiB of HBM per device.

v0:
```python
import functools
import math

import jax
import jax.numpy as jnp
from jax import lax
from jax.experimental import pallas as pl
from jax.experimental.pallas import tpu as pltpu
from jax.sharding import PartitionSpec as P

GROUP = 16
TEAM = 8
CHIPS = 4
PARTS = 6


def round_up(value, step):
    return (value + step - 1) // step * step


def remote(src, dst, send_sem, recv_sem, peer):
    return pltpu.make_async_remote_copy(
        src_ref=src,
        dst_ref=dst,
        send_sem=send_sem,
        recv_sem=recv_sem,
        device_id={"seq": peer},
        device_id_type=pl.DeviceIdType.MESH,
    )


def fused_kernel(
    n, scaling, x_ref, weight_ref, taps_ref, grad_ref,
    grad_inputs_ref, out_ref, grad_taps_ref,
    send_taps, send_gated, send_back, got_taps, got_gated, got_back,
    made_mixed, made_conv, made_taps, home_mixed, home_conv, home_taps,
    pad_gated, pad_back, send_cols, got_cols, left, key_rows, value_rows,
    proj, proj_all, made, got, weights,
    go_sems, come_sems, back_sems, home_sems, send_cols_sems, recv_cols_sems,
    send_sems, relay_sems, recv_sems, send_sum_sems, recv_sum_sems, weight_sems,
):
    f32, bf16 = jnp.float32, jnp.bfloat16
    me = lax.axis_index("seq")
    rows, depth = x_ref.shape
    channels = taps_ref.shape[1]
    width = 3 * channels // PARTS
    cpd = channels // n
    slim = send_taps.shape[0] // n
    teams = n // TEAM
    team, mine = me // TEAM, lax.rem(me, TEAM)
    base, chip, core = team * TEAM, mine // 2, lax.rem(mine, 2)
    sibling = chip * 2 + 1 - core
    block = depth // n
    share = depth // TEAM
    pieces = weight_sems.shape[0]
    piece = depth // pieces

    def slot(ref, index, height):
        return ref.at[pl.ds(pl.multiple_of(index * height, 8), height), :]

    def load(k):
        span = pl.ds(k * piece, piece)
        return pltpu.make_async_copy(
            weight_ref.at[span, :], weights.at[span, :], weight_sems.at[k]
        )

    for k in range(pieces):
        load(k).start()
    barrier = pltpu.get_barrier_semaphore()

    @pl.loop(1, n)
    def _(o):
        pl.semaphore_signal(
            barrier, inc=1, device_id={"seq": lax.rem(me + o, n)},
            device_id_type=pl.DeviceIdType.MESH,
        )

    def spread(ref, values):
        if slim == cpd:
            ref[...] = values
        else:
            for p in range(n):
                ref[p * slim : p * slim + cpd, :] = values[p * cpd : (p + 1) * cpd, :]

    def gather(ref):
        if slim == cpd:
            return ref[...]
        return jnp.concatenate([ref[p * slim : p * slim + cpd, :] for p in range(n)], axis=0)

    anti = (
        lax.broadcasted_iota(jnp.int32, (rows, rows), 0)
        + lax.broadcasted_iota(jnp.int32, (rows, rows), 1)
        == rows - 1
    ).astype(f32)

    def reverse(values):
        return jnp.dot(
            values, anti, preferred_element_type=f32, precision=lax.Precision.HIGHEST
        )

    spread(send_taps, taps_ref[...].T)
    for g in range(TEAM):
        for h in range(teams):
            first = (h * TEAM + g) * block
            send_cols[g * rows : (g + 1) * rows, h * block : (h + 1) * block] = x_ref[
                :, first : first + block
            ].astype(f32)
    pl.semaphore_wait(barrier, n - 1)

    def forth_taps(peer, sender):
        return (remote(slot(send_taps, peer, slim), slot(got_taps, sender, slim),
                       go_sems.at[0, peer], come_sems.at[0, sender], peer),)

    def forth(peer, sender):
        return (
            remote(slot(send_gated, peer, slim), slot(got_gated, sender, slim),
                   go_sems.at[1, peer], come_sems.at[1, sender], peer),
            remote(slot(send_back, peer, slim), slot(got_back, n - 1 - sender, slim),
                   go_sems.at[2, peer], come_sems.at[2, sender], peer),
        )

    def home(peer, sender):
        return (
            remote(slot(made_mixed, peer, slim), slot(home_mixed, sender, slim),
                   back_sems.at[0, peer], home_sems.at[0, sender], peer),
            remote(slot(made_conv, n - 1 - peer, slim), slot(home_conv, sender, slim),
                   back_sems.at[1, peer], home_sems.at[1, sender], peer),
        )

    def home_last(peer, sender):
        return (remote(slot(made_taps, n - 1 - peer, slim), slot(home_taps, sender, slim),
                       back_sems.at[2, peer], home_sems.at[2, sender], peer),)

    def exchange_start(plan):
        @pl.loop(1, n)
        def _(o):
            for copy in plan(lax.rem(me + o, n), me):
                copy.start()

    def exchange_wait(plan):
        @pl.loop(1, n)
        def _(o):
            other = lax.rem(me + n - o, n)
            for copy in plan(other, other):
                copy.wait_recv()

    def exchange_sent(plan):
        @pl.loop(1, n)
        def _(o):
            for copy in plan(lax.rem(me + o, n), me):
                copy.wait_send()

    def cols(target, sender, peer):
        return remote(slot(send_cols, target, rows), slot(got_cols, sender, rows),
                      send_cols_sems.at[target], recv_cols_sems.at[sender], base + peer)

    def cols_start(other):
        cols(other, mine, other).start()

    exchange_start(forth_taps)
    near = (chip + 1 - 2 * lax.rem(chip, 2)) * 2
    next_pair = lax.rem(chip + 2, CHIPS) * 2
    corner = lax.rem(chip + 3 - 2 * lax.rem(chip, 2), CHIPS) * 2
    cols_start(sibling)
    cols_start(near + core)
    cols_start(next_pair + core)
    total = jnp.zeros((rows, 3 * channels), f32)
    for k in range(pieces):
        load(k).wait()
        total = total + jnp.dot(
            x_ref[:, k * piece : (k + 1) * piece], weights[k * piece : (k + 1) * piece, :],
            preferred_element_type=f32,
        )
    total = total.astype(bf16).astype(f32)
    key_rows[...] = total[:, channels : 2 * channels]
    value_rows[...] = total[:, 2 * channels :]
    spread(send_gated, (total[:, channels : 2 * channels] * total[:, 2 * channels :]).T)
    spread(send_back, reverse((grad_ref[...].astype(f32) * total[:, :channels]).T))
    exchange_start(forth)
    cols_start(near + 1 - core)
    cols_start(next_pair + 1 - core)
    cols_start(corner + core)
    cols_start(corner + 1 - core)

    slot(got_cols, mine, rows)[...] = slot(send_cols, mine, rows)[...]
    slot(got_taps, me, slim)[...] = slot(send_taps, me, slim)[...]
    slot(got_gated, me, slim)[...] = slot(send_gated, me, slim)[...]
    slot(got_back, n - 1 - me, slim)[...] = slot(send_back, me, slim)[...]
    pad_gated[pl.ds(0, n), :] = jnp.zeros((n, rows), f32)
    pad_back[pl.ds(0, n), :] = jnp.zeros((n, rows), f32)
    exchange_wait(forth_taps)
    exchange_wait(forth)

    lane = lax.broadcasted_iota(jnp.int32, (rows, rows), 1)
    line = lax.broadcasted_iota(jnp.int32, (rows, rows), 0)
    keep = lane >= line
    group = min(GROUP, n)

    def turned(source, c, index):
        row = source[pl.ds(index * slim + c, 1), :]
        return pltpu.roll(
            jnp.broadcast_to(row, (rows, rows)), 0, 1, stride=1, stride_axis=0
        )

    def channel(c, carry):
        pad_gated[pl.ds(n, n), :] = got_gated[pl.ds(c, n, stride=slim), :]
        pad_back[pl.ds(n, n), :] = got_back[pl.ds(c, n, stride=slim), :]

        def some_lags(q, total):
            matrices = []
            for source in (got_taps, got_gated):
                if isinstance(q, int):
                    before = jnp.zeros((rows, rows), f32)
                else:
                    before = turned(source, c, jnp.maximum(q * group - 1, 0))
                    before = jnp.where(q == 0, 0.0, before)
                parts = []
                for e in range(group):
                    now = turned(source, c, q * group + e)
                    parts.append(jnp.where(keep, now, before).astype(bf16))
                    before = now
                matrices.append(jnp.concatenate(parts, axis=0))
            table = jnp.concatenate(matrices, axis=1)
            lines = jnp.concatenate(
                [
                    jnp.concatenate(
                        [pad[pl.ds(n - q * group - e, n), :] for e in range(group)], axis=1
                    ).astype(bf16)
                    for pad in (pad_gated, pad_back)
                ],
                axis=0,
            )
            return total + jnp.dot(lines, table, preferred_element_type=f32)

        sums = jnp.zeros((2 * n, 2 * rows), f32)
        if n == group:
            sums = some_lags(0, sums)
        else:
            sums = lax.fori_loop(0, n // group, some_lags, sums)
        made_mixed[pl.ds(c, n, stride=slim), :] = sums[:n, :rows]
        late = reverse(jnp.concatenate([sums[n:, :rows], sums[n:, rows:]], axis=0))
        made_conv[pl.ds(c, n, stride=slim), :] = late[:n]
        made_taps[pl.ds(c, n, stride=slim), :] = late[n:]
        return carry

    lax.fori_loop(0, cpd, channel, 0)
    exchange_start(home)
    slot(home_mixed, me, slim)[...] = slot(made_mixed, me, slim)[...]
    slot(home_conv, me, slim)[...] = slot(made_conv, n - 1 - me, slim)[...]
    slot(home_taps, me, slim)[...] = slot(made_taps, n - 1 - me, slim)[...]

    def held(part, member):
        return slot(proj_all, part * TEAM + member, rows)

    def own(part):
        return proj.at[pl.ds(part * rows, rows), :]

    def direct(part, o, sender, peer):
        return remote(own(part), held(part, sender), send_sems.at[part, o],
                      recv_sems.at[part, sender], base + peer)

    def relay(part, o, member):
        return remote(held(part, member), held(part, member), relay_sems.at[part, o],
                      recv_sems.at[part, member], base + sibling)

    def across(o):
        return lax.rem(chip + o, CHIPS) * 2 + core

    def sums_copy(part, to_team, from_team, peer):
        return remote(slot(made, part * teams + to_team, block),
                      slot(got, part * teams + from_team, block),
                      send_sum_sems.at[part, to_team], recv_sum_sems.at[part, from_team],
                      peer * TEAM + mine)

    exchange_wait(home)
    conv = gather(home_conv).T * scaling
    mixed = gather(home_mixed).T * scaling
    values = jnp.concatenate(
        [grad_ref[...].astype(f32) * mixed, conv * value_rows[...], conv * key_rows[...]], axis=1
    )
    for part in range(PARTS):
        rounded = values[:, part * width : (part + 1) * width].astype(bf16).astype(f32)
        own(part)[...] = rounded
        held(part, mine)[...] = rounded
    for part in range(PARTS):
        for o in range(1, CHIPS):
            direct(part, o, mine, across(o)).start()
        direct(part, 0, mine, sibling).start()
    exchange_start(home_last)

    @pl.loop(1, TEAM)
    def _(o):
        other = lax.rem(mine + o, TEAM)
        cols(other, mine, other).wait_send()
        cols(other, other, other).wait_recv()

    for s in range(TEAM):
        left[:, s * rows : (s + 1) * rows] = got_cols[s * rows : (s + 1) * rows, :].T.astype(bf16)
    tile = min(512, depth)

    def grad_inputs_tiles(first, last):
        lines = jnp.concatenate(
            [own(part)[...].astype(bf16) for part in range(PARTS)], axis=1
        )

        @pl.loop(first, last)
        def _(t):
            start = pl.multiple_of(t * tile, tile)
            grad_inputs_ref[:, pl.ds(start, tile)] = lax.dot_general(
                lines, weights[pl.ds(start, tile), :], (((1,), (1,)), ((), ())),
                preferred_element_type=f32,
            ).astype(bf16)

    for part in range(PARTS):
        for o in range(1, CHIPS):
            direct(part, o, across(o), across(o)).wait_recv()
            relay(part, o, across(o)).start()
        direct(part, 0, sibling, sibling).wait_recv()
        for o in range(1, CHIPS):
            relay(part, o, lax.rem(chip + o, CHIPS) * 2 + 1 - core).wait_recv()
        right = proj_all[part * TEAM * rows : (part + 1) * TEAM * rows, :].astype(bf16)

        def product(index):
            lines = left[pl.ds(pl.multiple_of(index * block, 16), block), :]
            return jnp.dot(lines, right, preferred_element_type=f32)

        def send_one(o, carry):
            target = lax.rem(team + o, teams)
            slot(made, part * teams + target, block)[...] = product(target)
            sums_copy(part, target, team, target).start()
            return carry

        lax.fori_loop(1, teams, send_one, 0)
        out_ref[:, part * width : (part + 1) * width] = product(team)

    grad_inputs_tiles(0, depth // tile)
    exchange_wait(home_last)
    grad_taps_ref[...] = gather(home_taps).T * scaling

    for part in range(PARTS):
        span = slice(part * width, (part + 1) * width)

        def add_one(o, carry):
            other = lax.rem(team + o, teams)
            sums_copy(part, other, other, other).wait_recv()
            out_ref[:, span] = out_ref[:, span] + slot(got, part * teams + other, block)[...]
            return carry

        lax.fori_loop(1, teams, add_one, 0)
        out_ref[:, span] = out_ref[:, span] * scaling

    for plan in (forth_taps, forth, home, home_last):
        exchange_sent(plan)
    for part in range(PARTS):
        for o in range(1, CHIPS):
            direct(part, o, mine, across(o)).wait_send()
            relay(part, o, across(o)).wait_send()
        direct(part, 0, mine, sibling).wait_send()

        def sent_one(o, carry):
            target = lax.rem(team + o, teams)
            sums_copy(part, target, team, target).wait_send()
            return carry

        lax.fori_loop(1, teams, sent_one, 0)


def write_kernel(*refs):
    sems = refs[-1]
    copies = [pltpu.make_async_copy(refs[k], refs[3 + k], sems.at[k]) for k in range(3)]
    for copy in copies:
        copy.start()
    for copy in copies:
        copy.wait()


def per_device(inputs, in_weight, filter_taps, grad_out):
    rows, depth = inputs.shape
    channels = filter_taps.shape[1]
    n = lax.axis_size("seq")
    scaling = 1.0 / math.sqrt(rows * n)
    slim = round_up(channels // n, 8)
    share = depth // TEAM
    width = 3 * channels // PARTS
    f32, bf16 = jnp.float32, jnp.bfloat16
    vmem = pl.BlockSpec(memory_space=pltpu.VMEM)
    dma = pltpu.SemaphoreType.DMA
    results = pl.pallas_call(
        functools.partial(fused_kernel, n, scaling),
        out_shape=(
            jax.ShapeDtypeStruct((rows, depth), bf16),
            jax.ShapeDtypeStruct((depth // n, 3 * channels), f32),
            jax.ShapeDtypeStruct((rows, channels), f32),
        ),
        in_specs=[vmem, pl.BlockSpec(memory_space=pl.ANY), vmem, vmem],
        out_specs=(vmem,) * 3,
        scratch_shapes=[pltpu.VMEM((n * slim, rows), f32)] * 12
        + [
            pltpu.VMEM((2 * n, rows), f32),
            pltpu.VMEM((2 * n, rows), f32),
            pltpu.VMEM((TEAM * rows, share), f32),
            pltpu.VMEM((TEAM * rows, share), f32),
            pltpu.VMEM((share, TEAM * rows), bf16),
            pltpu.VMEM((rows, channels), f32),
            pltpu.VMEM((rows, channels), f32),
            pltpu.VMEM((PARTS * rows, width), f32),
            pltpu.VMEM((PARTS * TEAM * rows, width), f32),
            pltpu.VMEM((PARTS * share, width), f32),
            pltpu.VMEM((PARTS * share, width), f32),
            pltpu.VMEM(in_weight.shape, in_weight.dtype),
            dma((3, n)), dma((3, n)), dma((3, n)), dma((3, n)), dma((TEAM,)), dma((TEAM,)),
            dma((PARTS, CHIPS)), dma((PARTS, CHIPS)), dma((PARTS, TEAM)),
            dma((PARTS, n // TEAM)), dma((PARTS, n // TEAM)), dma((4,)),
        ],
        compiler_params=pltpu.CompilerParams(
            collective_id=0, has_side_effects=True, vmem_limit_bytes=59 << 20
        ),
    )(inputs, in_weight, filter_taps, grad_out)
    return pl.pallas_call(
        write_kernel,
        out_shape=tuple(jax.ShapeDtypeStruct(r.shape, r.dtype) for r in results),
        in_specs=[vmem] * 3,
        out_specs=(pl.BlockSpec(memory_space=pl.ANY),) * 3,
        scratch_shapes=[dma((3,))],
        compiler_params=pltpu.CompilerParams(vmem_limit_bytes=8 << 20),
    )(*results)


def solution(mesh):
    in_specs = (P(("grp", "seq"), None), P(), P("seq", None), P(("grp", "seq"), None))
    out_specs = (P(("grp", "seq"), None), P(("grp", "seq"), None), P(("grp", "seq"), None))
    return jax.shard_map(
        per_device, mesh=mesh, in_specs=in_specs, out_specs=out_specs, check_vma=False
    )
```

profile of v0, /device:TPU:0, one launch (start us, length us, event | category | flops | bytes accessed | tf_op | source)
XLA Modules:
  0.0 97.3 jit_solution(1076557072331610986)
XLA Ops:
  0.6 92.1 %shard_map.67 = (bf16[128,4096]{1,0:T(8,128)(2,1)}, f32[256,768]{1,0:T(8,128)}, f32[128,256]{1,0:T(8,128)}) custom-call(bf16[128,4096]{1,0:T(8,128)(2,1)} %x_ref.1, bf16[4096,768]{1,0:T(8,128)(2,1)} %weight_ref.1, f32[128,256]{1,0:T(8,128)} %taps_ref.1, bf16[128,256]{1,0:T(8,128)(2,1)} %grad_ref.1), custom_call_target="tpu_custom_call" | custom-call | tf_op jit(solution)/shard_map/pallas_call | solution.py:388
  92.7 0.0 copy-start
  92.7 1.2 %copy-done = bf16[128,4096]{1,0:T(8,128)(2,1)S(1)} copy-done((bf16[128,4096]{1,0:T(8,128)(2,1)S(1)}, bf16[128,4096]{1,0:T(8,128)(2,1)}, u32[]{:S(2)}) %copy-start) | copy-done | bytes 1048600
  93.9 0.0 copy-start.1
  93.9 1.1 %copy-done.1 = f32[256,768]{1,0:T(8,128)S(1)} copy-done((f32[256,768]{1,0:T(8,128)S(1)}, f32[256,768]{1,0:T(8,128)}, u32[]{:S(2)}) %copy-start.1) | copy-done | bytes 786456
  95.1 0.0 copy-start.2
  95.1 0.9 copy-done.2
  96.0 1.3 %shard_map.68 = (bf16[128,4096]{1,0:T(8,128)(2,1)}, f32[256,768]{1,0:T(8,128)}, f32[128,256]{1,0:T(8,128)}) custom-call(bf16[128,4096]{1,0:T(8,128)(2,1)S(1)} %copy-done, f32[256,768]{1,0:T(8,128)S(1)} %copy-done.1, f32[128,256]{1,0:T(8,128)S(1)} %copy-done.2), custom_call_target="tpu_custom_call" | custom-call | tf_op jit(solution)/shard_map/pallas_call | solution.py:419
Async XLA Ops:
  92.7 1.2 %copy-start = (bf16[128,4096]{1,0:T(8,128)(2,1)S(1)}, bf16[128,4096]{1,0:T(8,128)(2,1)}, u32[]{:S(2)}) copy-start(bf16[128,4096]{1,0:T(8,128)(2,1)} %get-tuple-element.6.refs_0_) | copy-start | bytes 3145732
  93.9 1.1 %copy-start.1 = (f32[256,768]{1,0:T(8,128)S(1)}, f32[256,768]{1,0:T(8,128)}, u32[]{:S(2)}) copy-start(f32[256,768]{1,0:T(8,128)} %get-tuple-element.7.refs_1_) | copy-start | bytes 2359300
  95.1 0.9 copy-start.2
where the time goes:
time: 97.5 us; the launch traced here: 97.3 us
  Pallas kernels  93.3 us (96%)
  local copies, waits for them, and re-layouts  3.25 us (3%)
    pallas_call x1, Pallas kernels, per_device(): pl.pallas_call(functools.partial(fused_kernel, n, scaling), out_shape=(ja...  92.1 us
    unnamed x6, local copies, waits for them, and re-layouts  3.25 us

commit v1 on v0

v1 whole, which is shorter than its diff:
```python
import functools
import math

import jax
import jax.numpy as jnp
from jax import lax
from jax.experimental import pallas as pl
from jax.experimental.pallas import tpu as pltpu
from jax.sharding import PartitionSpec as P

GROUP = 16
TEAM = 8
CHIPS = 4
SUBLANES = 8
LANES = 128
PIECES = 4


def round_up(value, step):
    return (value + step - 1) // step * step


def chunks_of(per_device):
    return per_device // SUBLANES if per_device % SUBLANES == 0 else 1


def remote(src, dst, send_sem, recv_sem, peer):
    return pltpu.make_async_remote_copy(
        src_ref=src,
        dst_ref=dst,
        send_sem=send_sem,
        recv_sem=recv_sem,
        device_id={"seq": peer},
        device_id_type=pl.DeviceIdType.MESH,
    )


def fused_kernel(
    n, scaling, x_hbm, weight_hbm, taps_hbm, grad_hbm,
    grad_inputs_ref, out_ref, grad_taps_ref,
    x_ref, taps_ref, grad_ref, weights,
    send_taps, got_taps, send_pair, got_pair, back_rev, conv_rev,
    made_pair, home_pair, made_taps, home_taps,
    pad_gated, pad_back, send_cols, got_cols, left, key_rows, value_rows,
    proj_all, made, got,
    load_sems, weight_sems,
    taps_send, taps_recv, pair_send, pair_recv, home_send, home_recv, last_send, last_recv,
    cols_send, cols_recv, direct_send, relay_send, gather_recv, sums_send, sums_recv,
):
    f32, bf16 = jnp.float32, jnp.bfloat16
    me = lax.axis_index("seq")
    rows, depth = x_ref.shape
    channels = taps_ref.shape[1]
    cpd = channels // n
    chunks = chunks_of(cpd)
    own_channels = cpd // chunks
    slim = round_up(own_channels, SUBLANES)
    wide = channels // chunks
    parts = 3 * chunks
    teams = n // TEAM
    team, mine = me // TEAM, lax.rem(me, TEAM)
    base, chip, core = team * TEAM, mine // 2, lax.rem(mine, 2)
    near = (chip + 1 - 2 * lax.rem(chip, 2)) * 2
    far = lax.rem(chip + 2, CHIPS) * 2
    corner = (CHIPS - 1 - chip) * 2
    sibling = chip * 2 + 1 - core
    block = depth // n
    share = depth // TEAM
    cuts = teams if block % LANES == 0 else 1
    pieces = weight_sems.shape[0]
    piece = depth // pieces

    def slot(ref, index, height):
        return ref.at[pl.ds(pl.multiple_of(index * height, 8), height), :]

    def load(k):
        span = pl.ds(k * piece, piece)
        return pltpu.make_async_copy(
            weight_hbm.at[span, :], weights.at[span, :], weight_sems.at[k]
        )

    small = [
        pltpu.make_async_copy(src, dst, load_sems.at[k])
        for k, (src, dst) in enumerate(
            ((taps_hbm, taps_ref), (x_hbm, x_ref), (grad_hbm, grad_ref))
        )
    ]
    for copy in small:
        copy.start()
    for k in range(pieces):
        load(k).start()
    barrier = pltpu.get_barrier_semaphore()

    @pl.loop(1, n)
    def _(o):
        pl.semaphore_signal(
            barrier, inc=1, device_id={"seq": lax.rem(me + o, n)},
            device_id_type=pl.DeviceIdType.MESH,
        )

    anti = (
        lax.broadcasted_iota(jnp.int32, (rows, rows), 0)
        + lax.broadcasted_iota(jnp.int32, (rows, rows), 1)
        == rows - 1
    )

    def reverse(values):
        return jnp.dot(
            values, anti.astype(f32), preferred_element_type=f32,
            precision=lax.Precision.HIGHEST,
        )

    def turn(values):
        high = values.astype(bf16)
        low = (values - high.astype(f32)).astype(bf16)
        flip = anti.astype(bf16)
        over = (((1,), (1,)), ((), ()))
        return lax.dot_general(
            flip, high, over, preferred_element_type=f32
        ) + lax.dot_general(flip, low, over, preferred_element_type=f32)

    def spread(ref, values, start, step):
        for p in range(n):
            at = start + p * step
            ref[at : at + own_channels, :] = values[p * own_channels : (p + 1) * own_channels, :]

    def collect(ref, start, step):
        return jnp.concatenate(
            [ref[start + p * step : start + p * step + own_channels, :] for p in range(n)], axis=0
        )

    small[0].wait()
    lag_rows = taps_ref[...].T
    for k in range(chunks):
        spread(send_taps, lag_rows[k * wide : (k + 1) * wide], k * slim, chunks * slim)
    small[1].wait()
    for g in range(TEAM):
        for h in range(teams):
            first = (h * TEAM + g) * block
            send_cols[g * rows : (g + 1) * rows, h * block : (h + 1) * block] = x_ref[
                :, first : first + block
            ].astype(f32)
    pl.semaphore_wait(barrier, n - 1)

    def taps_plan(peer, sender):
        return remote(slot(send_taps, peer, chunks * slim), slot(got_taps, sender, chunks * slim),
                      taps_send.at[peer], taps_recv.at[sender], peer)

    def pair_plan(k):
        return lambda peer, sender: remote(
            slot(send_pair, k * n + peer, 2 * slim), slot(got_pair, k * n + sender, 2 * slim),
            pair_send.at[k, peer], pair_recv.at[k, sender], peer)

    def home_plan(k):
        return lambda peer, sender: remote(
            slot(made_pair, k * n + peer, 2 * slim), slot(home_pair, k * n + sender, 2 * slim),
            home_send.at[k, peer], home_recv.at[k, sender], peer)

    def last_plan(peer, sender):
        return remote(slot(made_taps, n - 1 - peer, chunks * slim),
                      slot(home_taps, sender, chunks * slim),
                      last_send.at[peer], last_recv.at[sender], peer)

    def exchange_start(plan):
        @pl.loop(1, n)
        def _(o):
            plan(lax.rem(me + o, n), me).start()

    def exchange_wait(plan, after=None):
        @pl.loop(1, n)
        def _(o):
            other = lax.rem(me + n - o, n)
            plan(other, other).wait_recv()
            if after is not None:
                after(other)

    def exchange_sent(plan):
        @pl.loop(1, n)
        def _(o):
            plan(lax.rem(me + o, n), me).wait_send()

    def cols_cut(ref, member, cut):
        if cuts == 1:
            return slot(ref, member, rows)
        return ref.at[
            pl.ds(pl.multiple_of(member * rows, 8), rows),
            pl.ds(pl.multiple_of(cut * block, LANES), block),
        ]

    def cols(target, sender, peer, cut):
        return remote(cols_cut(send_cols, target, cut), cols_cut(got_cols, sender, cut),
                      cols_send.at[target, cut], cols_recv.at[sender, cut], base + peer)

    def cols_start(other, first, last):
        for o in range(first, last):
            cols(other, mine, other, lax.rem(team + o, cuts) if cuts > 1 else 0).start()

    early = (1, cuts) if cuts > 1 else (0, 1)
    late = (cuts, cuts + 1) if cuts > 1 else (0, 0)

    exchange_start(taps_plan)
    for other in (sibling, near + core, far + core):
        cols_start(other, *early)
    small[2].wait()
    total = jnp.zeros((rows, 3 * channels), f32)
    for k in range(pieces):
        load(k).wait()
        total = total + jnp.dot(
            x_ref[:, k * piece : (k + 1) * piece], weights[k * piece : (k + 1) * piece, :],
            preferred_element_type=f32,
        )
    total = total.astype(bf16).astype(f32)
    key_rows[...] = total[:, channels : 2 * channels]
    value_rows[...] = total[:, 2 * channels :]
    gated = (total[:, channels : 2 * channels] * total[:, 2 * channels :]).T
    back = reverse((grad_ref[...].astype(f32) * total[:, :channels]).T)
    for k in range(chunks):
        spread(send_pair, gated[k * wide : (k + 1) * wide], k * n * 2 * slim, 2 * slim)
        spread(send_pair, back[k * wide : (k + 1) * wide], k * n * 2 * slim + slim, 2 * slim)
        exchange_start(pair_plan(k))
    for other in (near + 1 - core, far + 1 - core, corner + core, corner + 1 - core):
        cols_start(other, *early)

    slot(got_cols, mine, rows)[...] = slot(send_cols, mine, rows)[...]
    slot(got_taps, me, chunks * slim)[...] = slot(send_taps, me, chunks * slim)[...]
    for k in range(chunks):
        slot(got_pair, k * n + me, 2 * slim)[...] = slot(send_pair, k * n + me, 2 * slim)[...]
    unroll = pad_gated.shape[0]
    for u in range(unroll):
        pad_gated[u, pl.ds(0, n), :] = jnp.zeros((n, rows), f32)
        pad_back[u, pl.ds(0, n), :] = jnp.zeros((n, rows), f32)

    lane = lax.broadcasted_iota(jnp.int32, (rows, rows), 1)
    line = lax.broadcasted_iota(jnp.int32, (rows, rows), 0)
    keep = lane >= line
    group = min(GROUP, n)

    def turned(source, index):
        ref, start, step = source
        row = ref[pl.ds(start + index * step, 1), :]
        return pltpu.roll(
            jnp.broadcast_to(row, (rows, rows)), 0, 1, stride=1, stride_axis=0
        )

    def convolve(k, c, u):
        pair_start = k * n * 2 * slim + c
        back_start = k * n * slim + c
        pad_gated[u, pl.ds(n, n), :] = got_pair[pl.ds(pair_start, n, stride=2 * slim), :]
        pad_back[u, pl.ds(n, n), :] = back_rev[pl.ds(back_start, n, stride=slim), :]

        def some_lags(q, total):
            matrices = []
            for source in (
                (got_taps, k * slim + c, chunks * slim), (got_pair, pair_start, 2 * slim)
            ):
                if isinstance(q, int):
                    before = jnp.zeros((rows, rows), f32)
                else:
                    before = turned(source, jnp.maximum(q * group - 1, 0))
                    before = jnp.where(q == 0, 0.0, before)
                tiles = []
                for e in range(group):
                    now = turned(source, q * group + e)
                    tiles.append(jnp.where(keep, now, before).astype(bf16))
                    before = now
                matrices.append(jnp.concatenate(tiles, axis=0))
            table = jnp.concatenate(matrices, axis=1)
            lines = jnp.concatenate(
                [
                    jnp.concatenate(
                        [pad[u, pl.ds(n - q * group - e, n), :] for e in range(group)], axis=1
                    ).astype(bf16)
                    for pad in (pad_gated, pad_back)
                ],
                axis=0,
            )
            return total + jnp.dot(lines, table, preferred_element_type=f32)

        sums = jnp.zeros((2 * n, 2 * rows), f32)
        if n == group:
            sums = some_lags(0, sums)
        else:
            sums = lax.fori_loop(0, n // group, some_lags, sums)
        made_pair[pl.ds(pair_start, n, stride=2 * slim), :] = sums[:n, :rows]
        conv_rev[pl.ds(back_start, n, stride=slim), :] = sums[n:, :rows]
        made_taps[pl.ds(k * slim + c, n, stride=chunks * slim), :] = sums[n:, rows:]

    def back_rows(k, s):
        slot(back_rev, k * n + n - 1 - s, slim)[...] = got_pair[
            pl.ds(pl.multiple_of((k * n + s) * 2 * slim + slim, 8), slim), :
        ]

    exchange_wait(taps_plan)
    for k in range(chunks):
        back_rows(k, me)
        exchange_wait(pair_plan(k), functools.partial(back_rows, k))

        def channel_group(i, carry):
            for u in range(unroll):
                convolve(k, i * unroll + u, u)
            return carry

        lax.fori_loop(0, own_channels // unroll, channel_group, 0)

        @pl.loop(0, n)
        def _(r):
            made_pair[pl.ds(pl.multiple_of((k * n + n - 1 - r) * 2 * slim + slim, 8), slim), :] = (
                slot(conv_rev, k * n + r, slim)[...]
            )

        exchange_start(home_plan(k))
        slot(home_pair, k * n + me, 2 * slim)[...] = slot(made_pair, k * n + me, 2 * slim)[...]
    slot(home_taps, me, chunks * slim)[...] = slot(made_taps, n - 1 - me, chunks * slim)[...]

    def held(part, member):
        return slot(proj_all, part * TEAM + member, rows)

    def pass_on(part, member, sem, peer):
        return remote(held(part, member), held(part, member), sem,
                      gather_recv.at[part, member], base + peer)

    def directs(part):
        return [
            pass_on(part, mine, direct_send.at[part, i], peer)
            for i, peer in enumerate((far + core, near + core, sibling))
        ]

    def relays(part):
        return [
            pass_on(part, far + core, relay_send.at[part, 0], near + core),
            pass_on(part, far + core, relay_send.at[part, 1], sibling),
            pass_on(part, near + core, relay_send.at[part, 2], sibling),
            pass_on(part, corner + core, relay_send.at[part, 3], sibling),
        ]

    def arrived(part, member):
        pass_on(part, member, direct_send.at[part, 0], sibling).wait_recv()

    def project(k):
        exchange_wait(home_plan(k))
        start = k * n * 2 * slim
        mixed = collect(home_pair, start, 2 * slim).T * scaling
        conv = turn(collect(home_pair, start + slim, 2 * slim)) * scaling
        span = slice(k * wide, (k + 1) * wide)
        for j, values in enumerate((
            grad_ref[:, span].astype(f32) * mixed,
            conv * value_rows[:, span],
            conv * key_rows[:, span],
        )):
            held(3 * k + j, mine)[...] = values.astype(bf16).astype(f32)
        for j in range(3):
            for copy in directs(3 * k + j):
                copy.start()

    def cols_wait(first, last):
        @pl.loop(1, TEAM)
        def _(o):
            other = lax.rem(mine + o, TEAM)
            for t in range(first, last):
                cut = lax.rem(team + t, cuts) if cuts > 1 else 0
                cols(other, other, other, cut).wait_recv()

        for t in range(first, last):
            if cuts == 1:
                for s in range(TEAM):
                    left[:, s * rows : (s + 1) * rows] = (
                        got_cols[s * rows : (s + 1) * rows, :].T.astype(bf16)
                    )
            else:
                cut = lax.rem(team + t, cuts)
                for s in range(TEAM):
                    left[pl.ds(pl.multiple_of(cut * block, 16), block), s * rows : (s + 1) * rows] = (
                        got_cols[
                            s * rows : (s + 1) * rows,
                            pl.ds(pl.multiple_of(cut * block, LANES), block),
                        ].T.astype(bf16)
                    )

    def first_relays(k):
        for part in range(3 * k, 3 * k + 3):
            hops = relays(part)
            arrived(part, far + core)
            hops[0].start()
            hops[1].start()
            arrived(part, near + core)
            hops[2].start()

    def second_relays(k):
        for part in range(3 * k, 3 * k + 3):
            arrived(part, corner + core)
            relays(part)[3].start()

    def product(part, index):
        right = proj_all[part * TEAM * rows : (part + 1) * TEAM * rows, :].astype(bf16)
        lines = left[pl.ds(pl.multiple_of(index * block, 16), block), :]
        return jnp.dot(lines, right, preferred_element_type=f32)

    def sums_copy(part, to_team, from_team, peer):
        return remote(slot(made, part * teams + to_team, block),
                      slot(got, part * teams + from_team, block),
                      sums_send.at[part, to_team], sums_recv.at[part, from_team],
                      peer * TEAM + mine)

    def send_sums(k):
        for part in range(3 * k, 3 * k + 3):
            arrived(part, sibling)
            for other in (far + 1 - core, near + 1 - core, corner + 1 - core):
                arrived(part, other)

            def send_one(o, carry):
                target = lax.rem(team + o, teams)
                slot(made, part * teams + target, block)[...] = product(part, target)
                sums_copy(part, target, team, target).start()
                return carry

            lax.fori_loop(1, teams, send_one, 0)

    project(0)
    exchange_start(last_plan)
    for k in range(1, chunks):
        project(k)
    cols_wait(*early)
    for k in range(chunks):
        first_relays(k)
        second_relays(k)
        if k == chunks - 1:
            for other in (sibling, near + core, far + core, near + 1 - core, far + 1 - core,
                          corner + core, corner + 1 - core):
                cols_start(other, *late)
        send_sums(k)

    tile = min(512, depth)
    lines = jnp.concatenate(
        [held(3 * k + j, mine)[...].astype(bf16) for j in range(3) for k in range(chunks)], axis=1
    )

    @pl.loop(0, depth // tile)
    def _(t):
        start = pl.multiple_of(t * tile, tile)
        grad_inputs_ref[:, pl.ds(start, tile)] = lax.dot_general(
            lines, weights[pl.ds(start, tile), :], (((1,), (1,)), ((), ())),
            preferred_element_type=f32,
        ).astype(bf16)

    exchange_wait(last_plan)
    for k in range(chunks):
        grad_taps_ref[:, k * wide : (k + 1) * wide] = (
            turn(collect(home_taps, k * slim, chunks * slim)) * scaling
        )
    cols_wait(*late)

    def columns(part):
        k, j = part // 3, part % 3
        return slice(j * channels + k * wide, j * channels + (k + 1) * wide)

    for part in range(parts):
        out_ref[:, columns(part)] = product(part, team)
    for part in range(parts):
        def add_one(o, carry):
            other = lax.rem(team + o, teams)
            sums_copy(part, other, other, other).wait_recv()
            out_ref[:, columns(part)] = (
                out_ref[:, columns(part)] + slot(got, part * teams + other, block)[...]
            )
            return carry

        lax.fori_loop(1, teams, add_one, 0)
        out_ref[:, columns(part)] = out_ref[:, columns(part)] * scaling

    exchange_sent(taps_plan)
    for k in range(chunks):
        exchange_sent(pair_plan(k))
        exchange_sent(home_plan(k))
    exchange_sent(last_plan)

    @pl.loop(1, TEAM)
    def _(o):
        other = lax.rem(mine + o, TEAM)
        for cut in range(cuts):
            cols(other, mine, other, cut).wait_send()

    for part in range(parts):
        for copy in directs(part) + relays(part):
            copy.wait_send()

        def sent_one(o, carry):
            target = lax.rem(team + o, teams)
            sums_copy(part, target, team, target).wait_send()
            return carry

        lax.fori_loop(1, teams, sent_one, 0)


def write_kernel(*refs):
    sems = refs[-1]
    copies = [pltpu.make_async_copy(refs[k], refs[3 + k], sems.at[k]) for k in range(3)]
    for copy in copies:
        copy.start()
    for copy in copies:
        copy.wait()


def per_device(inputs, in_weight, filter_taps, grad_out):
    rows, depth = inputs.shape
    channels = filter_taps.shape[1]
    n = lax.axis_size("seq")
    scaling = 1.0 / math.sqrt(rows * n)
    cpd = channels // n
    chunks = chunks_of(cpd)
    own_channels = cpd // chunks
    slim = round_up(own_channels, SUBLANES)
    wide = channels // chunks
    parts = 3 * chunks
    teams = n // TEAM
    share = depth // TEAM
    cuts = teams if (depth // n) % LANES == 0 else 1
    unroll = math.gcd(own_channels, 4)
    f32, bf16 = jnp.float32, jnp.bfloat16
    vmem = pl.BlockSpec(memory_space=pltpu.VMEM)
    hbm = pl.BlockSpec(memory_space=pltpu.HBM)
    dma = pltpu.SemaphoreType.DMA
    signal = pltpu.VMEM((n * chunks * slim, rows), f32)
    pair = pltpu.VMEM((2 * n * chunks * slim, rows), f32)
    results = pl.pallas_call(
        functools.partial(fused_kernel, n, scaling),
        out_shape=(
            jax.ShapeDtypeStruct((rows, depth), bf16),
            jax.ShapeDtypeStruct((depth // n, 3 * channels), f32),
            jax.ShapeDtypeStruct((rows, channels), f32),
        ),
        in_specs=[hbm] * 4,
        out_specs=(vmem,) * 3,
        scratch_shapes=[
            pltpu.VMEM(inputs.shape, inputs.dtype),
            pltpu.VMEM(filter_taps.shape, filter_taps.dtype),
            pltpu.VMEM(grad_out.shape, grad_out.dtype),
            pltpu.VMEM(in_weight.shape, in_weight.dtype),
            signal, signal, pair, pair, signal, signal, pair, pair, signal, signal,
            pltpu.VMEM((unroll, 2 * n, rows), f32),
            pltpu.VMEM((unroll, 2 * n, rows), f32),
            pltpu.VMEM((TEAM * rows, share), f32),
            pltpu.VMEM((TEAM * rows, share), f32),
            pltpu.VMEM((share, TEAM * rows), bf16),
            pltpu.VMEM((rows, channels), f32),
            pltpu.VMEM((rows, channels), f32),
            pltpu.VMEM((parts * TEAM * rows, wide), f32),
            pltpu.VMEM((parts * share, wide), f32),
            pltpu.VMEM((parts * share, wide), f32),
            dma((3,)), dma((PIECES,)),
            dma((n,)), dma((n,)), dma((chunks, n)), dma((chunks, n)),
            dma((chunks, n)), dma((chunks, n)), dma((n,)), dma((n,)),
            dma((TEAM, cuts)), dma((TEAM, cuts)),
            dma((parts, 3)), dma((parts, 4)), dma((parts, TEAM)),
            dma((parts, teams)), dma((parts, teams)),
        ],
        compiler_params=pltpu.CompilerParams(
            collective_id=0, has_side_effects=True, vmem_limit_bytes=48 << 20
        ),
    )(*(pltpu.with_memory_space_constraint(a, pltpu.HBM)
        for a in (inputs, in_weight, filter_taps, grad_out)))
    return pl.pallas_call(
        write_kernel,
        out_shape=tuple(jax.ShapeDtypeStruct(r.shape, r.dtype) for r in results),
        in_specs=[vmem] * 3,
        out_specs=(pl.BlockSpec(memory_space=pl.ANY),) * 3,
        scratch_shapes=[dma((3,))],
        compiler_params=pltpu.CompilerParams(vmem_limit_bytes=8 << 20),
    )(*results)


def solution(mesh):
    in_specs = (P(("grp", "seq"), None), P(), P("seq", None), P(("grp", "seq"), None))
    out_specs = (P(("grp", "seq"), None), P(("grp", "seq"), None), P(("grp", "seq"), None))
    return jax.shard_map(
        per_device, mesh=mesh, in_specs=in_specs, out_specs=out_specs, check_vma=False
    )
```

time: 97.5 us -> 87.5 us (0.90)
  Pallas kernels: 93.3 us -> 86.7 us
  local copies, waits for them, and re-layouts: 3.25 us -> 0 us
    pallas_call x1, Pallas kernels: 92.1 us -> 85.5 us  [per_device(): pl.pallas_call(functools.partial(fused_kernel, n, scaling), out_shape=(ja...]
    unnamed x6 -> x0, local copies, waits for them, and re-layouts: 3.25 us -> none
where the time goes in v1:
time: 87.5 us; the launch traced here: 87.4 us
  Pallas kernels  86.7 us (99%)
    pallas_call x1, Pallas kernels, per_device(): pl.pallas_call(functools.partial(fused_kernel, n, scaling), out_shape=(ja...  85.5 us

profile of v1, /device:TPU:0, one launch (start us, length us, event | category | flops | bytes accessed | tf_op | source)
XLA Modules:
  0.0 87.4 jit_solution(8616919373129275509)
XLA Ops:
  0.6 85.5 %shard_map.67 = (bf16[128,4096]{1,0:T(8,128)(2,1)S(1)}, f32[256,768]{1,0:T(8,128)S(1)}, f32[128,256]{1,0:T(8,128)S(1)}) custom-call(bf16[128,4096]{1,0:T(8,128)(2,1)} %x_hbm.1, bf16[4096,768]{1,0:T(8,128)(2,1)} %weight_hbm.1, f32[128,256]{1,0:T(8,128)} %taps_hbm.1, bf16[128,256]{1,0:T(8,128)(2,1)} %grad_hbm.1), custom_call_target="tpu_custom_call" | custom-call | tf_op jit(solution)/shard_map/pallas_call | solution.py:524
  86.1 1.3 %shard_map.68 = (bf16[128,4096]{1,0:T(8,128)(2,1)}, f32[256,768]{1,0:T(8,128)}, f32[128,256]{1,0:T(8,128)}) custom-call(bf16[128,4096]{1,0:T(8,128)(2,1)S(1)} %get-tuple-element.6.refs_0_, f32[256,768]{1,0:T(8,128)S(1)} %get-tuple-element.7.refs_1_, f32[128,256]{1,0:T(8,128)S(1)} %get-tuple-element.8.refs_2_), custom_call_target="tpu_custom_call" | custom-call | tf_op jit(solution)/shard_map/pallas_call | solution.py:561
